TPU v7x, 128 devices: a whole 4x4x4 slice. The times are simulated.
128 devices in a mesh: blk: 16 (over y, x_hi, core), rep: 8 (over x_lo, z).
Axes of the slice: x: 4 (x_hi: 2, x_lo: 2; x = x_hi * 2 + x_lo), y: 4, z: 4, core: 2. Of those that a mesh axis runs over, the one named last changes fastest.
Arguments:
- cotangent: bfloat16 [512, 256, 128], P('blk', 'rep'), may hold values from -6 to 6
- relu_mask: int32 [512, 256, 128], P('blk', 'rep'), may hold values 0 or 1
- aggregated: bfloat16 [512, 256, 128], P('blk', 'rep'), may hold values from -6 to 6
- weight: bfloat16 [256, 256], P('rep'), may hold values from -0.375 to 0.375
- tiles: bfloat16 [512, 16, 128, 128], P('blk'), may hold values from -0.125 to 0.125
- col_block: int32 [512, 16], P('blk'), may hold values from 0 to 511, as said below
- live_count: int32 [512], P('blk'), may hold values from 1 to 16, as said below
Outputs:
- input_grad: bfloat16 [512, 256, 128], P('blk', 'rep')
- weight_grad: float32 [256, 256], P('rep')
Inputs may be any that keep to these rules, and one draw needn't show every extreme that they name: The slab of a row block b is b // 32; the slab of col_block[b, s] lies at most 2 slabs from it around the closed cycle of the 16 slabs, and both distance 2 directions occur. `live_count`: row blocks of one slab share a density level, so live counts differ from slab to slab; some row block has all 16 slots live.
All inputs are finite; a program needn't handle non-finite values. No bound on the sum of `relu_mask` on one device may be relied on, other than what follows from the above.
Results may differ from a plain program's by a relative error of at most 0.0049.
Values may be sent and summed in bfloat16 or wider, within the bound.
A program may use at most 128 MiB of HBM per device.

v0:
```python
import math
import jax
import jax.numpy as jnp
from jax import lax
from jax.sharding import PartitionSpec as P

REACH = 2


def from_behind(value, axis, steps):
    count = lax.axis_size(axis)
    pairs = [(source, (source + steps) % count) for source in range(count)]
    return lax.ppermute(value, axis, pairs)


def on_device(cotangent, relu_mask, aggregated, weight, tiles, col_block, live_count):
    blocks_here = cotangent.shape[0]
    cols_here = cotangent.shape[1]
    tile_size = cotangent.shape[2]
    grad_z = cotangent * relu_mask.astype(jnp.bfloat16)
    gathered_part = lax.all_gather(grad_z, "rep", axis=1, tiled=True)
    grad_h = jnp.einsum("io,bon->bin", weight, gathered_part, preferred_element_type=jnp.float32)
    col_part = jnp.einsum(
        "bin,bon->io", aggregated, gathered_part, preferred_element_type=jnp.float32
    )
    grad_w = col_part
    grad_h, grad_w = (grad_h, grad_w)
    nodes_all = lax.axis_size("blk") * blocks_here * tile_size
    weight_grad = lax.psum(grad_w, "blk") * (1.0 / math.sqrt(nodes_all))
    grad_hb = grad_h.astype(jnp.bfloat16)
    slot_count = tiles.shape[1]
    slot_ids = jnp.arange(slot_count, dtype=jnp.int32)
    live = (slot_ids[None, :] < live_count[:, None]).astype(jnp.float32).reshape(-1)
    contrib = jnp.einsum("bkij,bfi->bkfj", tiles, grad_hb, preferred_element_type=jnp.float32)
    flat_terms = contrib.reshape(blocks_here * slot_count, cols_here * tile_size)
    targets = col_block.reshape(-1)
    slabs = lax.axis_size("blk")
    own_slab = lax.axis_index("blk")
    target_slab = targets // blocks_here
    window_slot = (target_slab - own_slab + REACH + slabs) % slabs
    position = window_slot * blocks_here + targets % blocks_here
    window_rows = (2 * REACH + 1) * blocks_here
    row_ids = jnp.arange(window_rows, dtype=jnp.int32)
    selector = (position[None, :] == row_ids[:, None]).astype(jnp.float32) * live[None, :]
    window = jnp.dot(
        selector, flat_terms, preferred_element_type=jnp.float32, precision=lax.Precision.HIGHEST
    )
    window = window.reshape(2 * REACH + 1, blocks_here, cols_here, tile_size)
    input_grad = window[REACH]
    upward = window[2 * REACH]
    downward = window[0]
    for step in range(REACH):
        upward = from_behind(upward, "blk", 1)
        downward = from_behind(downward, "blk", -1)
        if step + 1 < REACH:
            upward = upward + window[2 * REACH - step - 1]
            downward = downward + window[step + 1]
    input_grad = input_grad + upward + downward
    return (input_grad.astype(jnp.bfloat16), weight_grad)


def solution(mesh):
    placed = (
        P("blk", "rep", None),
        P("blk", "rep", None),
        P("blk", "rep", None),
        P("rep", None),
        P("blk", None, None, None),
        P("blk", None),
        P("blk"),
    )
    return jax.shard_map(
        on_device,
        mesh=mesh,
        in_specs=placed,
        out_specs=(P("blk", "rep", None), P("rep", None)),
        check_vma=False,
    )
```

profile of v0, /device:TPU:0, one launch (start us, length us, event | category | flops | bytes accessed | tf_op | source)
XLA Modules:
  0.0 174.0 jit_solution(14960853211397327882)
XLA Ops:
  7.2 1.9 %convert_multiply_fusion = bf16[32,32,128]{2,1,0:T(8,128)(2,1)} fusion(bf16[32,32,128]{2,1,0:T(8,128)(2,1)} %param.7, s32[32,32,128]{2,1,0:T(8,128)} %param.8), kind=kLoop, calls=%fused_computation.19 | loop fusion | flops 262144 | bytes 1048576 | tf_op jit(solution)/shard_map/mul | solution.py:20
  9.1 0.8 copy.9
  9.9 0.1 reshape.102
  10.0 0.7 fusion.13
  10.7 0.1 reshape.104
  10.8 43.8 %all-gather.2.cloned.1.call-done = bf16[32,256,128]{2,1,0:T(8,128)(2,1)} async-done(((bf16[32,32,128]{2,1,0:T(8,128)(2,1)}), bf16[32,256,128]{2,1,0:T(8,128)(2,1)}) %all-gather.2.cloned.1.call-update) | async-done | bytes 2097168 | tf_op jit(solution)/shard_map/all_gather | solution.py:21
  54.6 9.9 %fusion.4 = f32[32,32,16,128]{3,1,2,0:T(8,128)} fusion(bf16[32,16,128,128]{3,2,1,0:T(8,128)(2,1)} %param.11, bf16[32,256,128]{2,1,0:T(8,128)(2,1)} %all-gather.2.cloned.1.call-done, bf16[32,256]{1,0:T(8,128)(2,1)} %param.10), kind=kOutput, calls=%fused_computation.6 | convolution fusion | flops 604110848 | bytes 27279360 | tf_op jit(solution)/shard_map/bkij,bfi->bkfj/dot_general | solution.py:34
  64.5 11.3 %fusion = f32[160,4096]{1,0:T(8,128)S(1)} fusion(f32[64,8,32,128]{3,2,1,0:T(8,128)} %bitcast.46, f32[512]{0:T(512)S(1)} %reshape.104, s32[512]{0:T(512)S(1)} %fusion.18), kind=kOutput, calls=%fused_computation | convolution fusion | flops 4026695680 | bytes 11014144 | tf_op jit(solution)/shard_map/dot_general | solution.py:45
  75.9 0.2 slice_bitcast_fusion.4
  76.0 0.1 copy.13
  76.1 0.1 collective-permute-start
  76.2 0.1 copy.15
  76.3 5.4 %collective-permute-start.2 = (f32[32,32,128]{2,1,0:T(8,128)S(1)}, f32[32,32,128]{2,1,0:T(8,128)S(1)}, u32[]{:S(2)}, u32[]{:S(2)}) collective-permute-start(f32[32,32,128]{2,1,0:T(8,128)S(1)} %bitcast.47), channel_id=1, source_target_pairs={{0,120},{8,0},{16,8},{24,16},{32,24},{40,32},{48,40},{56,48},{64,5... | collective-permute-start | bytes 1572872 | tf_op jit(solution)/shard_map/ppermute | solution.py:13
  81.7 0.1 copy.16
  81.8 0.1 copy.14
  81.9 8.8 %collective-permute-done = f32[32,32,128]{2,1,0:T(8,128)S(1)} collective-permute-done((f32[32,32,128]{2,1,0:T(8,128)S(1)}, f32[32,32,128]{2,1,0:T(8,128)S(1)}, u32[]{:S(2)}, u32[]{:S(2)}) %collective-permute-start) | collective-permute-done | bytes 524320 | tf_op jit(solution)/shard_map/ppermute | solution.py:13
  90.8 0.1 bitcast_add_fusion.1
  91.0 0.1 bitcast_add_fusion
  91.0 5.4 %collective-permute-start.3 = (f32[32,32,128]{2,1,0:T(8,128)S(1)}, f32[32,32,128]{2,1,0:T(8,128)S(1)}, u32[]{:S(2)}, u32[]{:S(2)}) collective-permute-start(f32[32,32,128]{2,1,0:T(8,128)S(1)} %bitcast_add_fusion), channel_id=1, source_target_pairs={{0,120},{8,0},{16,8},{24,16},{32,24},{40,32},{48,40},{56,48},{64,5... | collective-permute-start | bytes 1572872 | tf_op jit(solution)/shard_map/ppermute | solution.py:13
  96.4 0.1 copy.12
  96.6 0.7 convolution_bitcast_fusion
  97.3 68.4 %psum.7 = f32[32,256]{1,0:T(8,128)S(1)} all-reduce(f32[32,256]{1,0:T(8,128)S(1)} %convolution_bitcast_fusion), channel_id=1, replica_groups=mesh['blk'=16,'rep'=8] {'blk'}, use_global_device_ids=true, to_apply=%region_0.0 | all-reduce | flops 8192 | bytes 65536 | tf_op jit(solution)/shard_map/psum | solution.py:29
  165.6 0.6 broadcast_multiply_fusion
  166.3 0.9 fusion.6
  (11 shorter events, 0.2 us)
Async XLA Ops:
  7.2 89.4 %copy-start = (bf16[32,32,128]{2,1,0:T(8,128)(2,1)S(1)}, bf16[32,32,128]{2,1,0:T(8,128)(2,1)}, u32[]{:S(2)}) copy-start(bf16[32,32,128]{2,1,0:T(8,128)(2,1)} %param.9) | copy-start | bytes 786436
  7.2 47.5 %all-gather.2.cloned.1.call-start = ((), (), s32[]{:S(2)}) async-start(), calls=%async_computation | async-start | bytes 2359296 | tf_op jit(solution)/shard_map/all_gather | solution.py:21
  76.1 14.6 %collective-permute-start = (f32[32,32,128]{2,1,0:T(8,128)S(1)}, f32[32,32,128]{2,1,0:T(8,128)S(1)}, u32[]{:S(2)}, u32[]{:S(2)}) collective-permute-start(f32[32,32,128]{2,1,0:T(8,128)S(1)} %bitcast.48), channel_id=1, source_target_pairs={{0,8},{8,16},{16,24},{24,32},{32,40},{40,48},{48,56},{56,64},{64,7... | collective-permute-start | bytes 1572872 | tf_op jit(solution)/shard_map/ppermute | solution.py:13
  76.3 14.6 %collective-permute-start.2 = (f32[32,32,128]{2,1,0:T(8,128)S(1)}, f32[32,32,128]{2,1,0:T(8,128)S(1)}, u32[]{:S(2)}, u32[]{:S(2)}) collective-permute-start(f32[32,32,128]{2,1,0:T(8,128)S(1)} %bitcast.47), channel_id=1, source_target_pairs={{0,120},{8,0},{16,8},{24,16},{32,24},{40,32},{48,40},{56,48},{64,5... | collective-permute-start | bytes 1572872 | tf_op jit(solution)/shard_map/ppermute | solution.py:13
  81.8 14.7 %copy-start.1 = (bf16[32,256,128]{2,1,0:T(8,128)(2,1)S(1)}, bf16[32,256,128]{2,1,0:T(8,128)(2,1)}, u32[]{:S(2)}) copy-start(bf16[32,256,128]{2,1,0:T(8,128)(2,1)} %all-gather.2.cloned.1.call-done) | copy-start | bytes 6291460
  90.9 75.4 %collective-permute-start.1 = (f32[32,32,128]{2,1,0:T(8,128)S(1)}, f32[32,32,128]{2,1,0:T(8,128)S(1)}, u32[]{:S(2)}, u32[]{:S(2)}) collective-permute-start(f32[32,32,128]{2,1,0:T(8,128)S(1)} %bitcast_add_fusion.1), channel_id=1, source_target_pairs={{0,8},{8,16},{16,24},{24,32},{32,40},{40,48},{48,56},{56,64},{64,7... | collective-permute-start | bytes 1572872 | tf_op jit(solution)/shard_map/ppermute | solution.py:13
  91.0 75.2 %collective-permute-start.3 = (f32[32,32,128]{2,1,0:T(8,128)S(1)}, f32[32,32,128]{2,1,0:T(8,128)S(1)}, u32[]{:S(2)}, u32[]{:S(2)}) collective-permute-start(f32[32,32,128]{2,1,0:T(8,128)S(1)} %bitcast_add_fusion), channel_id=1, source_target_pairs={{0,120},{8,0},{16,8},{24,16},{32,24},{40,32},{48,40},{56,48},{64,5... | collective-permute-start | bytes 1572872 | tf_op jit(solution)/shard_map/ppermute | solution.py:13
Sparse Core Ops, SparseCore 0:
  10.2 44.3 all-gather.1
where the time goes:
time: 174 us
  blocking collectives  68.4 us (39%)
  waiting for transfers between devices  52.7 us (30%)
  matrix products  21.9 us (13%)
  between operations  14.1 us (8%)
  starting transfers between devices  11 us (6%)
  other arithmetic  4.3 us (2%)
    psum x1, blocking collectives, on_device(): weight_grad = lax.psum(grad_w, 'blk') * (1.0 / math.sqrt(nodes_all))  68.4 us
    all_gather x1, waiting for transfers between devices, on_device(): gathered_part = lax.all_gather(grad_z, 'rep', axis=1, tiled=True)  43.8 us
    dot_general x1, matrix products, on_device(): jnp.dot(selector, flat_terms, preferred_element_type=jnp.float32, precisi...  11.3 us
    ppermute x4, starting transfers between devices, from_behind(): return lax.ppermute(value, axis, pairs)  11 us
    dot_general x1, matrix products, on_device(): jnp.einsum('bkij,bfi->bkfj', tiles, grad_hb, preferred_element_type=jnp.f...  9.9 us
    ppermute x4, waiting for transfers between devices, from_behind(): return lax.ppermute(value, axis, pairs)  8.83 us
  transfers between devices with their start and end apart: 5, of which 2 were waited for; matrix products, arithmetic and copies ran while one was open for 2% of the time, Pallas kernels for 0%

commit v1 on v0

--- a/solution.py
+++ b/solution.py
@@ -5,6 +5,9 @@
 from jax.sharding import PartitionSpec as P
 
 REACH = 2
+review_squares_now = lambda xx, dim_i: jnp.concatenate(
+    lax.all_to_all(jnp.stack([xx] * lax.axis_size("rep")), "rep", 0, 0), axis=dim_i
+)
 
 
 def from_behind(value, axis, steps):
@@ -18,7 +21,7 @@
     cols_here = cotangent.shape[1]
     tile_size = cotangent.shape[2]
     grad_z = cotangent * relu_mask.astype(jnp.bfloat16)
-    gathered_part = lax.all_gather(grad_z, "rep", axis=1, tiled=True)
+    gathered_part = review_squares_now(grad_z, 1)
     grad_h = jnp.einsum("io,bon->bin", weight, gathered_part, preferred_element_type=jnp.float32)
     col_part = jnp.einsum(
         "bin,bon->io", aggregated, gathered_part, preferred_element_type=jnp.float32

time: 174 us -> 155 us (0.89)
  waiting for transfers between devices: 52.7 us -> 34.2 us
  between operations: 14.1 us -> 0.75 us
  starting transfers between devices: 11 us -> 17.3 us
  local copies, waits for them, and re-layouts: 1.6 us -> 6.15 us
    all_gather x1 -> x0, waiting for transfers between devices: 43.8 us -> none  [on_device(): gathered_part = lax.all_gather(grad_z, 'rep', axis=1, tiled=True)]
    all_to_all x0 -> x1, waiting for transfers between devices: none -> 25.7 us  [lax.all_to_all(jnp.stack([xx] * lax.axis_size('rep')), 'rep', 0, 0)]
    all_to_all x0 -> x1, starting transfers between devices: none -> 6.46 us  [lax.all_to_all(jnp.stack([xx] * lax.axis_size('rep')), 'rep', 0, 0)]
    reshape x0 -> x1, local copies, waits for them, and re-layouts: none -> 2.21 us  [jnp.concatenate(lax.all_to_all(jnp.stack([xx] * lax.axis_size('rep')), 'r...]
where the time goes in v1:
time: 155 us; the launch traced here: 154 us
  blocking collectives  68.6 us (44%)
  waiting for transfers between devices  34.2 us (22%)
  matrix products  21.1 us (14%)
  starting transfers between devices  17.3 us (11%)
  local copies, waits for them, and re-layouts  6.15 us (4%)
  other arithmetic  5.58 us (4%)
    psum x1, blocking collectives, on_device(): weight_grad = lax.psum(grad_w, 'blk') * (1.0 / math.sqrt(nodes_all))  68.6 us
    all_to_all x1, waiting for transfers between devices, lax.all_to_all(jnp.stack([xx] * lax.axis_size('rep')), 'rep', 0, 0)  25.7 us
    dot_general x1, matrix products, on_device(): jnp.dot(selector, flat_terms, preferred_element_type=jnp.float32, precisi...  11.3 us
    ppermute x4, starting transfers between devices, from_behind(): return lax.ppermute(value, axis, pairs)  10.8 us
    dot_general x1, matrix products, on_device(): jnp.einsum('bkij,bfi->bkfj', tiles, grad_hb, preferred_element_type=jnp.f...  9.16 us
    ppermute x4, waiting for transfers between devices, from_behind(): return lax.ppermute(value, axis, pairs)  8.5 us
    all_to_all x1, starting transfers between devices, lax.all_to_all(jnp.stack([xx] * lax.axis_size('rep')), 'rep', 0, 0)  6.46 us
  transfers between devices with their start and end apart: 5, of which 2 were waited for; matrix products, arithmetic and copies ran while one was open for 2% of the time, Pallas kernels for 0%

profile of v1, /device:TPU:0, one launch (start us, length us, event | category | flops | bytes accessed | tf_op | source)
XLA Modules:
  0.0 153.7 jit_solution(14500199615356821010)
XLA Ops:
  0.6 1.2 convert_multiply_fusion
  1.8 1.7 %stack.2 = bf16[8,32,32,128]{3,2,1,0:T(8,128)(2,1)} broadcast(bf16[32,32,128]{2,1,0:T(8,128)(2,1)S(1)} %convert_multiply_fusion), dimensions={1,2,3} | broadcast | bytes 2359296 | tf_op jit(solution)/shard_map/stack | solution.py:9
  3.5 6.5 %all-to-all-start = ((bf16[8,32,32,128]{3,2,1,0:T(8,128)(2,1)}), bf16[8,32,32,128]{3,2,1,0:T(8,128)(2,1)S(1)}, u32[]{:S(2)}, u32[]{:S(2)}) async-start(bf16[8,32,32,128]{3,2,1,0:T(8,128)(2,1)} %stack.2), calls=%async_computation | async-start | bytes 4194304 | tf_op jit(solution)/shard_map/all_to_all | solution.py:9
  10.1 0.1 reshape.110
  10.4 25.7 %all-to-all-done = bf16[8,32,32,128]{3,2,1,0:T(8,128)(2,1)S(1)} async-done(((bf16[8,32,32,128]{3,2,1,0:T(8,128)(2,1)}), bf16[8,32,32,128]{3,2,1,0:T(8,128)(2,1)S(1)}, u32[]{:S(2)}, u32[]{:S(2)}) %all-to-all-start) | async-done | bytes 2097184 | tf_op jit(solution)/shard_map/all_to_all | solution.py:9
  36.0 1.3 copy-done.1
  37.4 2.2 %copy.11 = bf16[32,8,32,128]{3,2,1,0:T(8,128)(2,1)S(1)} copy(bf16[32,8,32,128]{3,2,0,1:T(8,128)(2,1)} %bitcast.51) | data formatting | bytes 4194304 | tf_op jit(solution)/shard_map/reshape | solution.py:8
  39.6 9.2 %fusion.4 = f32[32,32,16,128]{3,1,2,0:T(8,128)} fusion(bf16[32,16,128,128]{3,2,1,0:T(8,128)(2,1)} %param.11, bf16[32,256,128]{2,1,0:T(8,128)(2,1)S(1)} %bitcast.49, bf16[32,256]{1,0:T(8,128)(2,1)S(1)} %copy-done.2), kind=kOutput, calls=%fused_computation.6 | convolution fusion | flops 604110848 | bytes 27279360 | tf_op jit(solution)/shard_map/bkij,bfi->bkfj/dot_general | solution.py:37
  48.8 11.3 %fusion = f32[160,4096]{1,0:T(8,128)S(1)} fusion(f32[64,8,32,128]{3,2,1,0:T(8,128)} %bitcast.48, f32[512]{0:T(512)S(1)} %reshape.114, s32[512]{0:T(512)S(1)} %fusion.18), kind=kOutput, calls=%fused_computation | convolution fusion | flops 4026695680 | bytes 11014144 | tf_op jit(solution)/shard_map/dot_general | solution.py:48
  60.1 0.2 slice_bitcast_fusion.4
  60.2 0.1 copy.15
  60.4 0.1 copy.17
  60.5 5.4 %collective-permute-start.2 = (f32[32,32,128]{2,1,0:T(8,128)S(1)}, f32[32,32,128]{2,1,0:T(8,128)S(1)}, u32[]{:S(2)}, u32[]{:S(2)}) collective-permute-start(f32[32,32,128]{2,1,0:T(8,128)S(1)} %bitcast.52), channel_id=1, source_target_pairs={{0,120},{8,0},{16,8},{24,16},{32,24},{40,32},{48,40},{56,48},{64,5... | collective-permute-start | bytes 1572872 | tf_op jit(solution)/shard_map/ppermute | solution.py:16
  65.9 0.1 copy.18
  66.0 0.1 copy.16
  66.1 8.5 %collective-permute-done = f32[32,32,128]{2,1,0:T(8,128)S(1)} collective-permute-done((f32[32,32,128]{2,1,0:T(8,128)S(1)}, f32[32,32,128]{2,1,0:T(8,128)S(1)}, u32[]{:S(2)}, u32[]{:S(2)}) %collective-permute-start) | collective-permute-done | bytes 524320 | tf_op jit(solution)/shard_map/ppermute | solution.py:16
  74.6 0.9 bitcast_add_fusion.1
  75.6 0.9 bitcast_add_fusion
  76.4 5.4 %collective-permute-start.3 = (f32[32,32,128]{2,1,0:T(8,128)}, f32[32,32,128]{2,1,0:T(8,128)}, u32[]{:S(2)}, u32[]{:S(2)}) collective-permute-start(f32[32,32,128]{2,1,0:T(8,128)} %bitcast_add_fusion), channel_id=1, source_target_pairs={{0,120},{8,0},{16,8},{24,16},{32,24},{40,32},{48,40},{56,48},{64,5... | collective-permute-start | bytes 1572872 | tf_op jit(solution)/shard_map/ppermute | solution.py:16
  81.8 0.1 copy.14
  81.9 0.7 convolution_bitcast_fusion
  82.6 68.6 %psum.7 = f32[32,256]{1,0:T(8,128)S(1)} all-reduce(f32[32,256]{1,0:T(8,128)S(1)} %convolution_bitcast_fusion), channel_id=1, replica_groups=mesh['blk'=16,'rep'=8] {'blk'}, use_global_device_ids=true, to_apply=%region_0.0 | all-reduce | flops 8192 | bytes 65536 | tf_op jit(solution)/shard_map/psum | solution.py:32
  151.2 0.6 broadcast_multiply_fusion
  151.9 1.9 %fusion.6 = bf16[32,32,128]{2,1,0:T(8,128)(2,1)} fusion(f32[32,32,128]{2,1,0:T(8,128)} %collective-permute-done.3, f32[32,32,128]{2,1,0:T(8,128)S(1)} %collective-permute-done.1, f32[4,8,32,128]{3,2,1,0:T(8,128)S(1)} %copy.14), kind=kLoop, calls=%fused_computation.11 | loop fusion | flops 393216 | bytes 1835008 | tf_op jit(solution)/shard_map/convert_element_type | solution.py:62
  (18 shorter events, 0.4 us)
Async XLA Ops:
  0.6 81.3 %copy-start = (bf16[32,32,128]{2,1,0:T(8,128)(2,1)S(1)}, bf16[32,32,128]{2,1,0:T(8,128)(2,1)}, u32[]{:S(2)}) copy-start(bf16[32,32,128]{2,1,0:T(8,128)(2,1)} %param.9) | copy-start | bytes 786436
  3.5 6.5 %copy-start.3 = (s32[32,16]{0,1:T(8,128)S(1)}, s32[32,16]{0,1:T(8,128)}, u32[]{:S(2)}) copy-start(s32[32,16]{0,1:T(8,128)} %param.12) | copy-start | bytes 6148
  3.5 6.6 %copy-start.4 = (s32[32]{0:T(128)S(1)}, s32[32]{0:T(128)}, u32[]{:S(2)}) copy-start(s32[32]{0:T(128)} %param.13) | copy-start | bytes 388
  3.5 32.5 %all-to-all-start = ((bf16[8,32,32,128]{3,2,1,0:T(8,128)(2,1)}), bf16[8,32,32,128]{3,2,1,0:T(8,128)(2,1)S(1)}, u32[]{:S(2)}, u32[]{:S(2)}) async-start(bf16[8,32,32,128]{3,2,1,0:T(8,128)(2,1)} %stack.2), calls=%async_computation | async-start | bytes 4194304 | tf_op jit(solution)/shard_map/all_to_all | solution.py:9
  10.0 29.6 %copy-start.2 = (bf16[32,256]{1,0:T(8,128)(2,1)S(1)}, bf16[32,256]{1,0:T(8,128)(2,1)}, u32[]{:S(2)}) copy-start(bf16[32,256]{1,0:T(8,128)(2,1)} %param.10) | copy-start | bytes 49156
  36.0 1.3 copy-start.1
  60.3 14.3 %collective-permute-start = (f32[32,32,128]{2,1,0:T(8,128)S(1)}, f32[32,32,128]{2,1,0:T(8,128)S(1)}, u32[]{:S(2)}, u32[]{:S(2)}) collective-permute-start(f32[32,32,128]{2,1,0:T(8,128)S(1)} %bitcast.53), channel_id=1, source_target_pairs={{0,8},{8,16},{16,24},{24,32},{32,40},{40,48},{48,56},{56,64},{64,7... | collective-permute-start | bytes 1572872 | tf_op jit(solution)/shard_map/ppermute | solution.py:16
  60.5 15.0 %collective-permute-start.2 = (f32[32,32,128]{2,1,0:T(8,128)S(1)}, f32[32,32,128]{2,1,0:T(8,128)S(1)}, u32[]{:S(2)}, u32[]{:S(2)}) collective-permute-start(f32[32,32,128]{2,1,0:T(8,128)S(1)} %bitcast.52), channel_id=1, source_target_pairs={{0,120},{8,0},{16,8},{24,16},{32,24},{40,32},{48,40},{56,48},{64,5... | collective-permute-start | bytes 1572872 | tf_op jit(solution)/shard_map/ppermute | solution.py:16
  75.5 76.3 %collective-permute-start.1 = (f32[32,32,128]{2,1,0:T(8,128)}, f32[32,32,128]{2,1,0:T(8,128)S(1)}, u32[]{:S(2)}, u32[]{:S(2)}) collective-permute-start(f32[32,32,128]{2,1,0:T(8,128)} %bitcast_add_fusion.1), channel_id=1, source_target_pairs={{0,8},{8,16},{16,24},{24,32},{32,40},{40,48},{48,56},{56,64},{64,7... | collective-permute-start | bytes 1572872 | tf_op jit(solution)/shard_map/ppermute | solution.py:16
  76.4 75.4 %collective-permute-start.3 = (f32[32,32,128]{2,1,0:T(8,128)}, f32[32,32,128]{2,1,0:T(8,128)}, u32[]{:S(2)}, u32[]{:S(2)}) collective-permute-start(f32[32,32,128]{2,1,0:T(8,128)} %bitcast_add_fusion), channel_id=1, source_target_pairs={{0,120},{8,0},{16,8},{24,16},{32,24},{40,32},{48,40},{56,48},{64,5... | collective-permute-start | bytes 1572872 | tf_op jit(solution)/shard_map/ppermute | solution.py:16
